TPU v7x, 32 devices: a whole 2x2x4 slice. The times are simulated.
32 devices in a mesh: section: 2 (over core), ctx: 8 (over z, x), tp: 2 (over y).
Axes of the slice: x: 2, y: 2, z: 4, core: 2. Of those that a mesh axis runs over, the one named last changes fastest.
Arguments:
- layer_input: bfloat16 [2, 1024, 1024], P(None, 'ctx'), may hold values from -6 to 6
- cotangent: bfloat16 [2, 1024, 1024], P(None, 'ctx'), may hold values from -6 to 6
- w_qkv: bfloat16 [2, 1024, 3, 1024], P('section', None, None, 'tp'), may hold values from -0.1875 to 0.1875
- b_qv: bfloat16 [2, 2, 1024], P('section', None, 'tp'), may hold values from -3 to 3
- w_out: bfloat16 [2, 1024, 1024], P('section', 'tp'), may hold values from -4 to 4
- b_out: bfloat16 [2, 1024], P('section'), may hold values from -3 to 3
- w_fc: bfloat16 [2, 1024, 4096], P('section', None, 'tp'), may hold values from -0.1875 to 0.1875
- b_fc: bfloat16 [2, 4096], P('section', 'tp'), may hold values from -3 to 3
- w_proj: bfloat16 [2, 4096, 1024], P('section', 'tp'), may hold values from -0.09375 to 0.09375
- b_proj: bfloat16 [2, 1024], P('section'), may hold values from -3 to 3
- ln_gain: float32 [2, 2, 1024], P('section'), may hold values from 0.5 to 1.5
- ln_bias: float32 [2, 2, 1024], P('section'), may hold values from -3 to 3
Outputs:
- activations: bfloat16 [2, 2, 1024, 1024], P('section', None, 'ctx')
- input_grads: float32 [2, 2, 1024, 1024], P('section', None, 'ctx')
- grad_w_qkv: float32 [2, 1024, 3, 1024], P('section', None, None, 'tp')
- grad_b_qv: float32 [2, 2, 1024], P('section', None, 'tp')
- grad_w_out: float32 [2, 1024, 1024], P('section', 'tp')
- grad_b_out: float32 [2, 1024], P('section')
- grad_w_fc: float32 [2, 1024, 4096], P('section', None, 'tp')
- grad_b_fc: float32 [2, 4096], P('section', 'tp')
- grad_w_proj: float32 [2, 4096, 1024], P('section', 'tp')
- grad_b_proj: float32 [2, 1024], P('section')
- grad_ln_gain: float32 [2, 2, 1024], P('section')
- grad_ln_bias: float32 [2, 2, 1024], P('section')
All inputs are finite; a program needn't handle non-finite values.
Results may differ from a plain program's by a relative error of at most 0.028.
Values may be sent and summed in bfloat16 or wider, within the bound.
A program may use at most 192 MiB of HBM per device.

v0:
```python
import jax
import jax.numpy as jnp
from jax import lax
from jax.sharding import PartitionSpec as P

HD = 64
EPS = 1e-05
GELU_C = 0.7978845608028654


def shifted(value, axis, steps):
    count = lax.axis_size(axis)
    first, last = (max(0, -steps), min(count, count - steps))
    return lax.ppermute(value, axis, [(source, source + steps) for source in range(first, last)])


def norm_forward(values, gain_vec, shift_vec):
    row_mean = jnp.mean(values, axis=-1, keepdims=True)
    centered = values - row_mean
    inv_std = lax.rsqrt(jnp.mean(centered * centered, axis=-1, keepdims=True) + EPS)
    normed = centered * inv_std
    return (normed * gain_vec + shift_vec, normed, inv_std)


def norm_backward(upstream, normed, inv_std, gain_vec):
    dnormed = upstream * gain_vec
    centered_grad = (
        dnormed
        - jnp.mean(dnormed, axis=-1, keepdims=True)
        - normed * jnp.mean(dnormed * normed, axis=-1, keepdims=True)
    )
    return (inv_std * centered_grad, jnp.sum(upstream * normed, axis=0), jnp.sum(upstream, axis=0))


def gelu_parts(pre_act):
    tanh_val = jnp.tanh(GELU_C * (pre_act + 0.044715 * pre_act * pre_act * pre_act))
    gelu_value = 0.5 * pre_act * (1.0 + tanh_val)
    gelu_slope = 0.5 * (1.0 + tanh_val) + 0.5 * pre_act * (1.0 - tanh_val * tanh_val) * GELU_C * (
        1.0 + 3.0 * 0.044715 * pre_act * pre_act
    )
    return (gelu_value, gelu_slope)


def split_heads(values, head_count):
    return values.reshape(values.shape[0], head_count, values.shape[1] // head_count)


def fold_keys(running, block_kv, queries, query_pos, head_count):
    totals, accum = running
    key_rows, val_rows = block_kv
    head_q = split_heads(queries, head_count)
    head_k = split_heads(key_rows, head_count)
    head_v = split_heads(val_rows, head_count)
    score_scale = HD ** (-0.5)
    scores = (
        jnp.einsum("qhd,khd->hqk", head_q, head_k, preferred_element_type=jnp.float32) * score_scale
    )
    key_pos = jnp.arange(key_rows.shape[0], dtype=jnp.int32)
    causal = query_pos[:, None] >= key_pos[None, :]
    weights = jnp.where(causal[None], jnp.exp(scores), 0.0)
    totals = jnp.sum(weights, axis=-1).T
    portion = jnp.einsum(
        "hqk,khd->qhd", weights.astype(jnp.bfloat16), head_v, preferred_element_type=jnp.float32
    )
    return (totals, portion.reshape(accum.shape))


def layer_forward(layer_in, weights_set, query_pos):
    w_qkv, b_qv, w_out, b_out, w_fc, b_fc, w_proj, b_proj, ln_gain, ln_bias = weights_set
    row_count, model_width = layer_in.shape
    local_cols = w_qkv.shape[2]
    head_count = local_cols // HD
    layer_f32 = layer_in.astype(jnp.float32)
    first_norm, normed_a, inv_a = norm_forward(layer_f32, ln_gain[0], ln_bias[0])
    first_bf = first_norm.astype(jnp.bfloat16)
    joined = jnp.dot(
        first_bf, w_qkv.reshape(model_width, 3 * local_cols), preferred_element_type=jnp.float32
    )
    queries = (joined[:, :local_cols] + b_qv[0].astype(jnp.float32)).astype(jnp.bfloat16)
    key_rows = joined[:, local_cols : 2 * local_cols].astype(jnp.bfloat16)
    val_rows = (joined[:, 2 * local_cols :] + b_qv[1].astype(jnp.float32)).astype(jnp.bfloat16)
    init_state = (
        jnp.zeros((row_count, head_count), jnp.float32),
        jnp.zeros((row_count, local_cols), jnp.float32),
    )
    totals, accum = fold_keys(
        init_state,
        (
            lax.all_gather(key_rows, "ctx", axis=0, tiled=True),
            lax.all_gather(val_rows, "ctx", axis=0, tiled=True),
        ),
        queries,
        query_pos,
        head_count,
    )
    held_keys = (key_rows, val_rows)
    attended = (
        (accum.reshape(row_count, head_count, HD) / totals[:, :, None])
        .reshape(row_count, local_cols)
        .astype(jnp.bfloat16)
    )
    log_total = jnp.log(totals)
    attn_mixed = lax.psum(
        jnp.dot(attended, w_out, preferred_element_type=jnp.float32).astype(jnp.bfloat16), "tp"
    ).astype(jnp.float32)
    hidden_in = layer_f32 + attn_mixed + b_out.astype(jnp.float32)
    second_norm, normed_b, inv_b = norm_forward(hidden_in, ln_gain[1], ln_bias[1])
    second_bf = second_norm.astype(jnp.bfloat16)
    pre_act = jnp.dot(second_bf, w_fc, preferred_element_type=jnp.float32) + b_fc.astype(
        jnp.float32
    )
    gelu_value, gelu_slope = gelu_parts(pre_act)
    act_bf = gelu_value.astype(jnp.bfloat16)
    mlp_mixed = lax.psum(
        jnp.dot(act_bf, w_proj, preferred_element_type=jnp.float32).astype(jnp.bfloat16), "tp"
    ).astype(jnp.float32)
    result = hidden_in + mlp_mixed + b_proj.astype(jnp.float32)
    saved = (
        normed_a,
        inv_a,
        first_bf,
        queries,
        (key_rows, val_rows),
        held_keys,
        attended,
        log_total,
        normed_b,
        inv_b,
        second_bf,
        act_bf,
        gelu_slope,
    )
    return (result.astype(jnp.bfloat16), saved)


def layer_backward(upstream, saved, weights_set, query_pos):
    w_qkv, b_qv, w_out, b_out, w_fc, b_fc, w_proj, b_proj, ln_gain, ln_bias = weights_set
    (
        normed_a,
        inv_a,
        first_bf,
        queries,
        own_kv,
        held_keys,
        attended,
        log_total,
        normed_b,
        inv_b,
        second_bf,
        act_bf,
        gelu_slope,
    ) = saved
    row_count, model_width = upstream.shape
    local_cols = w_qkv.shape[2]
    head_count = local_cols // HD
    score_scale = HD ** (-0.5)
    up_bf = upstream.astype(jnp.bfloat16)
    grad_b_proj = jnp.sum(upstream, axis=0)
    grad_w_proj = jnp.dot(act_bf.T, up_bf, preferred_element_type=jnp.float32)
    d_pre = jnp.dot(up_bf, w_proj.T, preferred_element_type=jnp.float32) * gelu_slope
    d_pre_bf = d_pre.astype(jnp.bfloat16)
    grad_b_fc = jnp.sum(d_pre, axis=0)
    grad_w_fc = jnp.dot(second_bf.T, d_pre_bf, preferred_element_type=jnp.float32)
    d_second = lax.psum(
        jnp.dot(d_pre_bf, w_fc.T, preferred_element_type=jnp.float32).astype(jnp.bfloat16), "tp"
    ).astype(jnp.float32)
    d_hidden_ln, gain_b, shift_b = norm_backward(d_second, normed_b, inv_b, ln_gain[1])
    d_hidden = upstream + d_hidden_ln
    grad_b_out = jnp.sum(d_hidden, axis=0)
    hidden_bf = d_hidden.astype(jnp.bfloat16)
    grad_w_out = jnp.dot(attended.T, hidden_bf, preferred_element_type=jnp.float32)
    d_attended = jnp.dot(hidden_bf, w_out.T, preferred_element_type=jnp.float32).astype(
        jnp.bfloat16
    )
    all_keys, all_vals = (
        lax.all_gather(held_keys[0], "ctx", axis=0, tiled=True),
        lax.all_gather(held_keys[1], "ctx", axis=0, tiled=True),
    )
    head_q = split_heads(queries, head_count)
    head_k = split_heads(all_keys, head_count)
    head_v = split_heads(all_vals, head_count)
    head_d = split_heads(d_attended, head_count)
    scores = (
        jnp.einsum("qhd,khd->hqk", head_q, head_k, preferred_element_type=jnp.float32) * score_scale
    )
    key_pos = jnp.arange(all_keys.shape[0], dtype=jnp.int32)
    causal = query_pos[:, None] >= key_pos[None, :]
    probs = jnp.where(causal[None], jnp.exp(scores - log_total.T[:, :, None]), 0.0)
    row_delta = jnp.sum(
        d_attended.astype(jnp.float32).reshape(row_count, head_count, HD)
        * attended.astype(jnp.float32).reshape(row_count, head_count, HD),
        axis=-1,
    )
    d_probs = jnp.einsum("qhd,khd->hqk", head_d, head_v, preferred_element_type=jnp.float32)
    d_scores = (probs * (d_probs - row_delta.T[:, :, None])).astype(jnp.bfloat16)
    d_query = (
        jnp.einsum("hqk,khd->qhd", d_scores, head_k, preferred_element_type=jnp.float32).reshape(
            row_count, local_cols
        )
        * score_scale
    )
    key_term = (
        jnp.einsum("hqk,qhd->khd", d_scores, head_q, preferred_element_type=jnp.float32).reshape(
            all_keys.shape[0], local_cols
        )
        * score_scale
    )
    val_term = jnp.einsum(
        "hqk,qhd->khd", probs.astype(jnp.bfloat16), head_d, preferred_element_type=jnp.float32
    ).reshape(all_keys.shape[0], local_cols)
    d_key, d_val = (
        lax.psum_scatter(
            key_term.astype(jnp.bfloat16), "ctx", scatter_dimension=0, tiled=True
        ).astype(jnp.float32),
        lax.psum_scatter(
            val_term.astype(jnp.bfloat16), "ctx", scatter_dimension=0, tiled=True
        ).astype(jnp.float32),
    )
    grad_b_qv = jnp.stack([jnp.sum(d_query, axis=0), jnp.sum(d_val, axis=0)])
    d_joined = jnp.concatenate([d_query, d_key, d_val], axis=1).astype(jnp.bfloat16)
    grad_w_qkv = jnp.dot(first_bf.T, d_joined, preferred_element_type=jnp.float32).reshape(
        model_width, 3, local_cols
    )
    d_first = lax.psum(
        jnp.dot(
            d_joined,
            w_qkv.reshape(model_width, 3 * local_cols).T,
            preferred_element_type=jnp.float32,
        ).astype(jnp.bfloat16),
        "tp",
    ).astype(jnp.float32)
    d_in_ln, gain_a, shift_a = norm_backward(d_first, normed_a, inv_a, ln_gain[0])
    d_input = d_hidden + d_in_ln
    grads = (
        grad_w_qkv,
        grad_b_qv,
        grad_w_out,
        grad_b_out,
        grad_w_fc,
        grad_b_fc,
        grad_w_proj,
        grad_b_proj,
        jnp.stack([gain_a, gain_b]),
        jnp.stack([shift_a, shift_b]),
    )
    return (d_input, grads)


def body(
    layer_input, cotangent, w_qkv, b_qv, w_out, b_out, w_fc, b_fc, w_proj, b_proj, ln_gain, ln_bias
):
    weights_set = (
        w_qkv[0],
        b_qv[0],
        w_out[0],
        b_out[0],
        w_fc[0],
        b_fc[0],
        w_proj[0],
        b_proj[0],
        ln_gain[0],
        ln_bias[0],
    )
    later_segment = lax.axis_index("section") == 1
    micro, row_count, model_width = layer_input.shape
    query_pos = lax.axis_index("ctx") * row_count + jnp.arange(row_count, dtype=jnp.int32)
    incoming = jnp.zeros((row_count, model_width), jnp.bfloat16)
    results = []
    saved_ticks = []
    for tick_index in range(micro + 1):
        if tick_index < micro:
            fresh_input = layer_input[tick_index]
        else:
            fresh_input = jnp.zeros((row_count, model_width), jnp.bfloat16)
        layer_in = jnp.where(later_segment, incoming, fresh_input)
        result, saved = layer_forward(layer_in, weights_set, query_pos)
        results.append(result)
        saved_ticks.append(saved)
        if tick_index < micro:
            incoming = shifted(result, "section", 1)
    outgoing = jnp.zeros((row_count, model_width), jnp.float32)
    grad_totals = []
    input_grads_all = []
    for tick_index in range(micro + 1):
        if tick_index < micro:
            given_grad = cotangent[tick_index].astype(jnp.float32)
        else:
            given_grad = jnp.zeros((row_count, model_width), jnp.float32)
        upstream = jnp.where(later_segment, given_grad, outgoing)
        saved = jax.tree.map(
            lambda late_val, early_val: jnp.where(later_segment, late_val, early_val),
            saved_ticks[min(tick_index + 1, micro)],
            saved_ticks[max(tick_index - 1, 0)],
        )
        d_input, grads = layer_backward(upstream, saved, weights_set, query_pos)
        if tick_index == 0:
            grad_totals = grads
        else:
            grad_totals = jax.tree.map(jnp.add, grad_totals, grads)
        input_grads_all.append(d_input)
        if tick_index < micro:
            outgoing = shifted(d_input.astype(jnp.bfloat16), "section", -1).astype(d_input.dtype)
    activations = jnp.stack(
        [
            jnp.where(later_segment, results[batch_index + 1], results[batch_index])
            for batch_index in range(micro)
        ]
    )[None]
    input_grads = jnp.stack(
        [
            jnp.where(later_segment, input_grads_all[batch_index], input_grads_all[batch_index + 1])
            for batch_index in range(micro)
        ]
    )[None]
    summed = (
        lax.psum(grad_totals[0].astype(jnp.bfloat16), "ctx").astype(jnp.float32),
        lax.psum(grad_totals[1].astype(jnp.bfloat16), "ctx").astype(jnp.float32),
        lax.psum(grad_totals[2].astype(jnp.bfloat16), "ctx").astype(jnp.float32),
        lax.psum(grad_totals[3].astype(jnp.bfloat16), "ctx").astype(jnp.float32),
        lax.psum(grad_totals[4].astype(jnp.bfloat16), "ctx").astype(jnp.float32),
        lax.psum(grad_totals[5].astype(jnp.bfloat16), "ctx").astype(jnp.float32),
        lax.psum(grad_totals[6].astype(jnp.bfloat16), "ctx").astype(jnp.float32),
        lax.psum(grad_totals[7].astype(jnp.bfloat16), "ctx").astype(jnp.float32),
        lax.psum(grad_totals[8].astype(jnp.bfloat16), "ctx").astype(jnp.float32),
        lax.psum(grad_totals[9].astype(jnp.bfloat16), "ctx").astype(jnp.float32),
    )
    return (
        activations,
        input_grads,
        summed[0][None],
        summed[1][None],
        summed[2][None],
        summed[3][None],
        summed[4][None],
        summed[5][None],
        summed[6][None],
        summed[7][None],
        summed[8][None],
        summed[9][None],
    )


def solution(mesh):
    placed = (
        P(None, "ctx", None),
        P(None, "ctx", None),
        P("section", None, None, "tp"),
        P("section", None, "tp"),
        P("section", "tp", None),
        P("section", None),
        P("section", None, "tp"),
        P("section", "tp"),
        P("section", "tp", None),
        P("section", None),
        P("section", None, None),
        P("section", None, None),
    )
    return jax.shard_map(
        body,
        mesh=mesh,
        in_specs=placed,
        out_specs=(
            P("section", None, "ctx", None),
            P("section", None, "ctx", None),
            P("section", None, None, "tp"),
            P("section", None, "tp"),
            P("section", "tp", None),
            P("section", None),
            P("section", None, "tp"),
            P("section", "tp"),
            P("section", "tp", None),
            P("section", None),
            P("section", None, None),
            P("section", None, None),
        ),
        check_vma=False,
    )
```

profile of v0, /device:TPU:0, one launch (start us, length us, event | category | flops | bytes accessed | tf_op | source)
XLA Modules:
  0.0 1655.5 jit_solution(18073447266085569030)
XLA Ops:
  21.0 42.0 %all-gather.15.cloned.1.call-done = bf16[1024,512]{1,0:T(8,128)(2,1)} async-done(((bf16[128,512]{1,0:T(8,128)(2,1)}), bf16[1024,512]{1,0:T(8,128)(2,1)}) %all-gather.15.cloned.1.call-update) | async-done | bytes 1048592 | tf_op jit(solution)/shard_map/all_gather | solution.py:89
  69.6 34.5 %all-gather.13.cloned.1.call-done = bf16[1024,512]{1,0:T(8,128)(2,1)} async-done(((bf16[128,512]{1,0:T(8,128)(2,1)}), bf16[1024,512]{1,0:T(8,128)(2,1)}) %all-gather.13.cloned.1.call-update) | async-done | bytes 1048592 | tf_op jit(solution)/shard_map/all_gather | solution.py:90
  109.9 22.1 %all-reduce.16.cloned.1.call-done = bf16[128,1024]{1,0:T(8,128)(2,1)} async-done(((bf16[128,1024]{1,0:T(8,128)(2,1)}), bf16[128,1024]{1,0:T(8,128)(2,1)}) %all-reduce.16.cloned.1.call-update) | async-done | bytes 262160 | tf_op jit(solution)/shard_map/psum | solution.py:103
  139.4 23.4 %all-reduce.18.cloned.1.call-done = bf16[128,1024]{1,0:T(8,128)(2,1)} async-done(((bf16[128,1024]{1,0:T(8,128)(2,1)}), bf16[128,1024]{1,0:T(8,128)(2,1)}) %all-reduce.18.cloned.1.call-update) | async-done | bytes 262160 | tf_op jit(solution)/shard_map/psum | solution.py:114
  173.6 39.7 %all-gather.19.cloned.1.call-done = bf16[1024,512]{1,0:T(8,128)(2,1)} async-done(((bf16[128,512]{1,0:T(8,128)(2,1)}), bf16[1024,512]{1,0:T(8,128)(2,1)}) %all-gather.19.cloned.1.call-update) | async-done | bytes 1048592 | tf_op jit(solution)/shard_map/all_gather | solution.py:89
  220.6 33.7 %all-gather.17.cloned.1.call-done = bf16[1024,512]{1,0:T(8,128)(2,1)} async-done(((bf16[128,512]{1,0:T(8,128)(2,1)}), bf16[1024,512]{1,0:T(8,128)(2,1)}) %all-gather.17.cloned.1.call-update) | async-done | bytes 1048592 | tf_op jit(solution)/shard_map/all_gather | solution.py:90
  261.6 21.6 %all-reduce.20.cloned.1.call-done = bf16[128,1024]{1,0:T(8,128)(2,1)} async-done(((bf16[128,1024]{1,0:T(8,128)(2,1)}), bf16[128,1024]{1,0:T(8,128)(2,1)}) %all-reduce.20.cloned.1.call-update) | async-done | bytes 262160 | tf_op jit(solution)/shard_map/psum | solution.py:103
  297.9 28.0 %all-reduce.34.cloned.1.call-done = (bf16[128,1024]{1,0:T(8,128)(2,1)}, bf16[128,1024]{1,0:T(8,128)(2,1)}) async-done(((bf16[128,1024]{1,0:T(8,128)(2,1)}, bf16[128,1024]{1,0:T(8,128)(2,1)}), (bf16[128,1024]{1,0:T(8,128)(2,1)}, bf16[128,1024]{1,0:T(8,128)(2,1)})) %all-reduce.34.cloned.1.call-update) | async-done | bytes 524304 | tf_op jit(solution)/shard_map/psum | solution.py:164
  338.4 30.5 %all-gather.25.cloned.1.call-done = bf16[1024,512]{1,0:T(8,128)(2,1)} async-done(((bf16[128,512]{1,0:T(8,128)(2,1)}), bf16[1024,512]{1,0:T(8,128)(2,1)}) %all-gather.25.cloned.1.call-update) | async-done | bytes 1048592 | tf_op jit(solution)/shard_map/all_gather | solution.py:176
  381.8 28.1 %all-gather.23.cloned.1.call-done = bf16[1024,512]{1,0:T(8,128)(2,1)} async-done(((bf16[128,512]{1,0:T(8,128)(2,1)}), bf16[1024,512]{1,0:T(8,128)(2,1)}) %all-gather.23.cloned.1.call-update) | async-done | bytes 1048592 | tf_op jit(solution)/shard_map/all_gather | solution.py:89
  422.1 28.9 %all-gather.27.cloned.1.call-done = bf16[1024,512]{1,0:T(8,128)(2,1)} async-done(((bf16[128,512]{1,0:T(8,128)(2,1)}), bf16[1024,512]{1,0:T(8,128)(2,1)}) %all-gather.27.cloned.1.call-update) | async-done | bytes 1048592 | tf_op jit(solution)/shard_map/all_gather | solution.py:177
  464.2 27.8 %all-gather.21.cloned.1.call-done = bf16[1024,512]{1,0:T(8,128)(2,1)} async-done(((bf16[128,512]{1,0:T(8,128)(2,1)}), bf16[1024,512]{1,0:T(8,128)(2,1)}) %all-gather.21.cloned.1.call-update) | async-done | bytes 1048592 | tf_op jit(solution)/shard_map/all_gather | solution.py:90
  500.4 58.6 %reduce-scatter.21.cloned.1.call-done = bf16[128,512]{1,0:T(8,128)(2,1)} async-done(((bf16[1024,512]{1,0:T(8,128)(2,1)}), bf16[128,512]{1,0:T(8,128)(2,1)}) %reduce-scatter.21.cloned.1.call-update) | async-done | bytes 131088
  560.1 65.4 %reduce-scatter.19.cloned.1.call-done = bf16[128,512]{1,0:T(8,128)(2,1)} async-done(((bf16[1024,512]{1,0:T(8,128)(2,1)}), bf16[128,512]{1,0:T(8,128)(2,1)}) %reduce-scatter.19.cloned.1.call-update) | async-done | bytes 131088
  631.6 26.0 %all-reduce.32.cloned.1.call-done = (bf16[128,1024]{1,0:T(8,128)(2,1)}, bf16[128,1024]{1,0:T(8,128)(2,1)}) async-done(((bf16[128,1024]{1,0:T(8,128)(2,1)}, bf16[128,1024]{1,0:T(8,128)(2,1)}), (bf16[128,1024]{1,0:T(8,128)(2,1)}, bf16[128,1024]{1,0:T(8,128)(2,1)})) %all-reduce.32.cloned.1.call-update) | async-done | bytes 524304 | tf_op jit(solution)/shard_map/psum | solution.py:224
  677.7 22.7 %all-gather.29.cloned.1.call-done = bf16[1024,512]{1,0:T(8,128)(2,1)} async-done(((bf16[128,512]{1,0:T(8,128)(2,1)}), bf16[1024,512]{1,0:T(8,128)(2,1)}) %all-gather.29.cloned.1.call-update) | async-done | bytes 1048592 | tf_op jit(solution)/shard_map/all_gather | solution.py:176
  706.7 18.5 %all-reduce.22.cloned.1.call-done = bf16[128,1024]{1,0:T(8,128)(2,1)} async-done(((bf16[128,1024]{1,0:T(8,128)(2,1)}), bf16[128,1024]{1,0:T(8,128)(2,1)}) %all-reduce.22.cloned.1.call-update) | async-done | bytes 262160 | tf_op jit(solution)/shard_map/psum | solution.py:164
  738.7 28.7 %all-gather.31.cloned.1.call-done = bf16[1024,512]{1,0:T(8,128)(2,1)} async-done(((bf16[128,512]{1,0:T(8,128)(2,1)}), bf16[1024,512]{1,0:T(8,128)(2,1)}) %all-gather.31.cloned.1.call-update) | async-done | bytes 1048592 | tf_op jit(solution)/shard_map/all_gather | solution.py:177
  795.2 13.4 all-gather.33.cloned.1.call-done
  810.9 38.7 %all-gather.35.cloned.1.call-done = bf16[1024,512]{1,0:T(8,128)(2,1)} async-done(((bf16[128,512]{1,0:T(8,128)(2,1)}), bf16[1024,512]{1,0:T(8,128)(2,1)}) %all-gather.35.cloned.1.call-update) | async-done | bytes 1048592 | tf_op jit(solution)/shard_map/all_gather | solution.py:177
  858.3 57.7 %reduce-scatter.25.cloned.1.call-done = bf16[128,512]{1,0:T(8,128)(2,1)} async-done(((bf16[1024,512]{1,0:T(8,128)(2,1)}), bf16[128,512]{1,0:T(8,128)(2,1)}) %reduce-scatter.25.cloned.1.call-update) | async-done | bytes 131088
  917.6 65.0 %reduce-scatter.23.cloned.1.call-done = bf16[128,512]{1,0:T(8,128)(2,1)} async-done(((bf16[1024,512]{1,0:T(8,128)(2,1)}), bf16[128,512]{1,0:T(8,128)(2,1)}) %reduce-scatter.23.cloned.1.call-update) | async-done | bytes 131088
  993.1 17.1 %all-reduce.24.cloned.1.call-done = bf16[128,1024]{1,0:T(8,128)(2,1)} async-done(((bf16[128,1024]{1,0:T(8,128)(2,1)}), bf16[128,1024]{1,0:T(8,128)(2,1)}) %all-reduce.24.cloned.1.call-update) | async-done | bytes 262160 | tf_op jit(solution)/shard_map/psum | solution.py:224
  1033.3 17.6 %all-reduce.26.cloned.1.call-done = bf16[128,1024]{1,0:T(8,128)(2,1)} async-done(((bf16[128,1024]{1,0:T(8,128)(2,1)}), bf16[128,1024]{1,0:T(8,128)(2,1)}) %all-reduce.26.cloned.1.call-update) | async-done | bytes 262160 | tf_op jit(solution)/shard_map/psum | solution.py:164
  1084.5 9.6 fusion.30
  1094.1 9.2 fusion.31
  1107.2 22.2 %reduce-scatter.29.cloned.1.call-done = bf16[128,512]{1,0:T(8,128)(2,1)} async-done(((bf16[1024,512]{1,0:T(8,128)(2,1)}), bf16[128,512]{1,0:T(8,128)(2,1)}) %reduce-scatter.29.cloned.1.call-update) | async-done | bytes 131088
  1130.5 65.4 %reduce-scatter.27.cloned.1.call-done = bf16[128,512]{1,0:T(8,128)(2,1)} async-done(((bf16[1024,512]{1,0:T(8,128)(2,1)}), bf16[128,512]{1,0:T(8,128)(2,1)}) %reduce-scatter.27.cloned.1.call-update) | async-done | bytes 131088
  1200.3 7.5 add_convert_fusion.2
  1230.8 39.5 %all-reduce = (bf16[1,2,512]{2,1,0:T(2,128)(2,1)S(1)}, bf16[1,1024]{1,0:T(2,128)(2,1)S(1)}, bf16[1,2048]{1,0:T(2,128)(2,1)S(1)}, bf16[1,1024]{1,0:T(2,128)(2,1)S...) all-reduce(bf16[1,2,512]{2,1,0:T(2,128)(2,1)S(1)} %fusion.327, ...), channel_id=1, replica_groups=mesh['section'=2,'ctx'=8,'tp'=2] {'ctx'}, use_global_device_ids=true, to_apply=%region_55.56 | all-reduce | flops 9216 | bytes 36864 | tf_op jit(solution)/shard_map/psum | solution.py:317
  1279.3 349.7 %all-reduce.28.cloned.1.call-done = (bf16[1,1024,3,512]{1,3,2,0:T(8,128)(2,1)}, bf16[1,512,1024]{2,1,0:T(8,128)(2,1)}, bf16[1,1024,2048]{2,1,0:T(8,128)(2,1)}, bf16[1,2048,1024]{2,1,0:T(8,128)(2,1)}) async-done(((bf16[1,1024,3,512]{1,3,2,0:T(8,128)(2,1)}, bf16[1,512,1024]{2,1,0:T(8,128)(2,1)}, bf16[1,1024,2048]{2,1,0:T(8,128)(2,1)}, bf16[1,2048,1024]{2,1,0:T(8,128)(2,1)}), ...) | async-done | bytes 12582928 | tf_op jit(solution)/shard_map/psum | solution.py:316
  1637.2 6.8 broadcast_in_dim.177
  (557 shorter events, 339.2 us)
Async XLA Ops:
  7.2 55.7 %all-gather.15.cloned.1.call-start = ((), (), s32[]{:S(2)}) async-start(), calls=%async_computation.7 | async-start | bytes 1179648 | tf_op jit(solution)/shard_map/all_gather | solution.py:89
  19.8 84.3 %all-gather.13.cloned.1.call-start = ((), (), s32[]{:S(2)}) async-start(), calls=%async_computation.6 | async-start | bytes 1179648 | tf_op jit(solution)/shard_map/all_gather | solution.py:90
  20.6 111.3 %all-reduce.16.cloned.1.call-start = ((), (), s32[]{:S(2)}) async-start(), calls=%async_computation.8 | async-start | bytes 524288 | tf_op jit(solution)/shard_map/psum | solution.py:103
  109.8 53.0 %all-reduce.18.cloned.1.call-start = ((), (), s32[]{:S(2)}) async-start(), calls=%async_computation.9 | async-start | bytes 524288 | tf_op jit(solution)/shard_map/psum | solution.py:114
  139.4 73.9 %all-gather.19.cloned.1.call-start = ((), (), s32[]{:S(2)}) async-start(), calls=%async_computation.11 | async-start | bytes 1179648 | tf_op jit(solution)/shard_map/all_gather | solution.py:89
  163.9 2.4 collective-permute-start
  172.8 81.4 %all-gather.17.cloned.1.call-start = ((), (), s32[]{:S(2)}) async-start(), calls=%async_computation.10 | async-start | bytes 1179648 | tf_op jit(solution)/shard_map/all_gather | solution.py:90
  173.4 109.8 %all-reduce.20.cloned.1.call-start = ((), (), s32[]{:S(2)}) async-start(), calls=%async_computation.12 | async-start | bytes 524288 | tf_op jit(solution)/shard_map/psum | solution.py:103
  261.0 64.9 %all-reduce.34.cloned.1.call-start = ((), (), s32[]{:S(2)}) async-start(), calls=%async_computation.33 | async-start | bytes 1048576 | tf_op jit(solution)/shard_map/psum | solution.py:164
  297.1 71.8 %all-gather.25.cloned.1.call-start = ((), (), s32[]{:S(2)}) async-start(), calls=%async_computation.15 | async-start | bytes 1179648 | tf_op jit(solution)/shard_map/all_gather | solution.py:176
  297.8 112.1 %all-gather.23.cloned.1.call-start = ((), (), s32[]{:S(2)}) async-start(), calls=%async_computation.14 | async-start | bytes 1179648 | tf_op jit(solution)/shard_map/all_gather | solution.py:89
  327.8 2.7 collective-permute-start.1
  336.6 114.4 %all-gather.27.cloned.1.call-start = ((), (), s32[]{:S(2)}) async-start(), calls=%async_computation.16 | async-start | bytes 1179648 | tf_op jit(solution)/shard_map/all_gather | solution.py:177
  337.4 154.7 %all-gather.21.cloned.1.call-start = ((), (), s32[]{:S(2)}) async-start(), calls=%async_computation.13 | async-start | bytes 1179648 | tf_op jit(solution)/shard_map/all_gather | solution.py:90
  375.2 183.8 %reduce-scatter.21.cloned.1.call-start = ((), (), s32[]{:S(2)}) async-start(), calls=%async_computation.25 | async-start | bytes 1179648
  421.9 203.6 %reduce-scatter.19.cloned.1.call-start = ((), (), s32[]{:S(2)}) async-start(), calls=%async_computation.24 | async-start | bytes 1179648
  464.2 193.4 %all-reduce.32.cloned.1.call-start = ((), (), s32[]{:S(2)}) async-start(), calls=%async_computation.32 | async-start | bytes 1048576 | tf_op jit(solution)/shard_map/psum | solution.py:224
  629.8 70.6 %all-gather.29.cloned.1.call-start = ((), (), s32[]{:S(2)}) async-start(), calls=%async_computation.18 | async-start | bytes 1179648 | tf_op jit(solution)/shard_map/all_gather | solution.py:176
  631.5 93.6 %all-reduce.22.cloned.1.call-start = ((), (), s32[]{:S(2)}) async-start(), calls=%async_computation.17 | async-start | bytes 524288 | tf_op jit(solution)/shard_map/psum | solution.py:164
  663.0 6.9 collective-permute-start.2
  675.4 92.1 %all-gather.31.cloned.1.call-start = ((), (), s32[]{:S(2)}) async-start(), calls=%async_computation.19 | async-start | bytes 1179648 | tf_op jit(solution)/shard_map/all_gather | solution.py:177
  676.1 132.5 %all-gather.33.cloned.1.call-start = ((), (), s32[]{:S(2)}) async-start(), calls=%async_computation.22 | async-start | bytes 1179648 | tf_op jit(solution)/shard_map/all_gather | solution.py:176
  676.9 172.7 %all-gather.35.cloned.1.call-start = ((), (), s32[]{:S(2)}) async-start(), calls=%async_computation.23 | async-start | bytes 1179648 | tf_op jit(solution)/shard_map/all_gather | solution.py:177
  677.5 238.5 %reduce-scatter.25.cloned.1.call-start = ((), (), s32[]{:S(2)}) async-start(), calls=%async_computation.27 | async-start | bytes 1179648
  738.7 243.9 %reduce-scatter.23.cloned.1.call-start = ((), (), s32[]{:S(2)}) async-start(), calls=%async_computation.26 | async-start | bytes 1179648
  780.6 229.5 %all-reduce.24.cloned.1.call-start = ((), (), s32[]{:S(2)}) async-start(), calls=%async_computation.20 | async-start | bytes 524288 | tf_op jit(solution)/shard_map/psum | solution.py:224
  987.7 63.3 %all-reduce.26.cloned.1.call-start = ((), (), s32[]{:S(2)}) async-start(), calls=%async_computation.21 | async-start | bytes 524288 | tf_op jit(solution)/shard_map/psum | solution.py:164
  1015.3 5.3 collective-permute-start.3
  1026.7 102.7 %reduce-scatter.29.cloned.1.call-start = ((), (), s32[]{:S(2)}) async-start(), calls=%async_computation.29 | async-start | bytes 1179648
  1065.1 130.8 %reduce-scatter.27.cloned.1.call-start = ((), (), s32[]{:S(2)}) async-start(), calls=%async_computation.28 | async-start | bytes 1179648
  1084.3 143.6 %all-reduce.30.cloned.1.call-start = ((), (), s32[]{:S(2)}) async-start(), calls=%async_computation.31 | async-start | bytes 1048576 | tf_op jit(solution)/shard_map/psum | solution.py:114
  1200.2 428.9 %all-reduce.28.cloned.1.call-start = ((), (), s32[]{:S(2)}) async-start(), calls=%async_computation.30 | async-start | bytes 25165824 | tf_op jit(solution)/shard_map/psum | solution.py:316
  (153 other events, 3767.6 us)
Sparse Core Ops, SparseCore 0:
  19.9 42.9 all-gather.14
  65.1 38.9 all-gather.12
  109.9 21.9 all-reduce.15
  139.5 23.2 all-reduce.17
  173.0 40.2 all-gather.18
  215.3 38.9 all-gather.16
  261.2 21.9 all-reduce.19
  297.2 28.6 all-reduce.33
  328.6 40.2 all-gather.24
  370.9 38.9 all-gather.22
  412.0 38.9 all-gather.26
  453.0 38.9 all-gather.20
  496.0 62.9 reduce-scatter.20
  562.3 63.1 reduce-scatter.18
  629.9 27.6 all-reduce.31
  660.1 40.2 all-gather.28
  703.1 21.9 all-reduce.21
  727.1 40.2 all-gather.30
  769.6 38.9 all-gather.32
  810.6 38.9 all-gather.34
  853.0 62.8 reduce-scatter.24
  919.3 63.2 reduce-scatter.22
  987.8 22.3 all-reduce.23
  1026.8 24.0 all-reduce.25
  1065.2 64.1 reduce-scatter.28
  1132.7 63.1 reduce-scatter.26
  1200.3 27.6 all-reduce.29
  1233.9 395.0 all-reduce.27
where the time goes:
time: 1670 us; the launch traced here: 1660 us
  waiting for transfers between devices  1240 us (74%)
  matrix products  188 us (11%)
  local copies, waits for them, and re-layouts  87.3 us (5%)
  other arithmetic  77.7 us (5%)
  blocking collectives  39.5 us (2%)
    psum x1, waiting for transfers between devices, body(): lax.psum(grad_totals[0].astype(jnp.bfloat16), 'ctx').astype(jnp.float32)  350 us
    unnamed x34, waiting for transfers between devices  338 us
    all_gather x3, waiting for transfers between devices, layer_forward(): lax.all_gather(key_rows, 'ctx', axis=0, tiled=True)  110 us
    all_gather x3, waiting for transfers between devices, layer_backward(): lax.all_gather(held_keys[1], 'ctx', axis=0, tiled=True)  96.4 us
    all_gather x3, waiting for transfers between devices, layer_forward(): lax.all_gather(val_rows, 'ctx', axis=0, tiled=True)  96 us
    all_gather x3, waiting for transfers between devices, layer_backward(): lax.all_gather(held_keys[0], 'ctx', axis=0, tiled=True)  66.6 us
    psum x3, waiting for transfers between devices, layer_backward(): lax.psum(jnp.dot(d_pre_bf, w_fc.T, preferred_element_type=jnp.float32).as...  64.1 us
    psum x2, waiting for transfers between devices, layer_forward(): lax.psum(jnp.dot(attended, w_out, preferred_element_type=jnp.float32).ast...  43.7 us
  transfers between devices with their start and end apart: 32, of which 30 were waited for; matrix products, arithmetic and copies ran while one was open for 14% of the time, Pallas kernels for 0%

commit v1 on v0

--- a/solution.py
+++ b/solution.py
@@ -1,11 +1,21 @@
+import functools
 import jax
 import jax.numpy as jnp
 from jax import lax
 from jax.sharding import PartitionSpec as P
+from jax.lax import all_gather
 
 HD = 64
 EPS = 1e-05
 GELU_C = 0.7978845608028654
+
+
+def _place_rounds(unit, mesh_ax):
+    base_arr = all_gather(unit, mesh_ax).sum(axis=0)
+    return base_arr
+
+
+finish_cubes = functools.partial(_place_rounds, mesh_ax="ctx")
 
 
 def shifted(value, axis, steps):
@@ -313,7 +323,7 @@
         ]
     )[None]
     summed = (
-        lax.psum(grad_totals[0].astype(jnp.bfloat16), "ctx").astype(jnp.float32),
+        finish_cubes(grad_totals[0].astype(jnp.bfloat16)).astype(jnp.float32),
         lax.psum(grad_totals[1].astype(jnp.bfloat16), "ctx").astype(jnp.float32),
         lax.psum(grad_totals[2].astype(jnp.bfloat16), "ctx").astype(jnp.float32),
         lax.psum(grad_totals[3].astype(jnp.bfloat16), "ctx").astype(jnp.float32),

time: 1670 us -> 2040 us (1.22)
  waiting for transfers between devices: 1240 us -> 1600 us
    all_gather x0 -> x1, waiting for transfers between devices: none -> 467 us  [_place_rounds(): base_arr = all_gather(unit, mesh_ax).sum(axis=0)]
    psum x1, waiting for transfers between devices: 350 us -> 249 us  [body(): lax.psum(grad_totals[2].astype(jnp.bfloat16), 'ctx').astype(jnp.float32)]
    psum x3 -> x2, waiting for transfers between devices: 64.1 us -> 37 us  [layer_backward(): lax.psum(jnp.dot(d_pre_bf, w_fc.T, preferred_element_type=jnp.float32).as...]
    psum x2 -> x3, waiting for transfers between devices: 43.7 us -> 69.7 us  [layer_forward(): lax.psum(jnp.dot(attended, w_out, preferred_element_type=jnp.float32).ast...]
    psum x2 -> x3, waiting for transfers between devices: 28.7 us -> 51.4 us  [layer_forward(): lax.psum(jnp.dot(act_bf, w_proj, preferred_element_type=jnp.float32).asty...]
    psum x2 -> x1, waiting for transfers between devices: 43.1 us -> 21.7 us  [layer_backward(): lax.psum(jnp.dot(d_joined, w_qkv.reshape(model_width, 3 * local_cols).T,...]
    unnamed x34 -> x35, waiting for transfers between devices: 338 us -> 345 us
    unnamed x320 -> x349, local copies, waits for them, and re-layouts: 42.3 us -> 46.1 us
  transfers between devices with their start and end apart: 32 -> 33, of which waited for: 30 -> 31; matrix products, arithmetic and copies ran while one was open for 14% -> 13% of each run, Pallas kernels for 0% -> 0%
where the time goes in v1:
time: 2040 us; the launch traced here: 2030 us
  waiting for transfers between devices  1600 us (78%)
  matrix products  171 us (8%)
  other arithmetic  96.9 us (5%)
  local copies, waits for them, and re-layouts  96.2 us (5%)
  blocking collectives  37.3 us (2%)
    all_gather x1, waiting for transfers between devices, _place_rounds(): base_arr = all_gather(unit, mesh_ax).sum(axis=0)  467 us
    unnamed x35, waiting for transfers between devices  345 us
    psum x1, waiting for transfers between devices, body(): lax.psum(grad_totals[2].astype(jnp.bfloat16), 'ctx').astype(jnp.float32)  249 us
    all_gather x3, waiting for transfers between devices, layer_forward(): lax.all_gather(key_rows, 'ctx', axis=0, tiled=True)  109 us
    all_gather x3, waiting for transfers between devices, layer_forward(): lax.all_gather(val_rows, 'ctx', axis=0, tiled=True)  96.6 us
    all_gather x3, waiting for transfers between devices, layer_backward(): lax.all_gather(held_keys[1], 'ctx', axis=0, tiled=True)  79.5 us
    psum x3, waiting for transfers between devices, layer_forward(): lax.psum(jnp.dot(attended, w_out, preferred_element_type=jnp.float32).ast...  69.7 us
    all_gather x3, waiting for transfers between devices, layer_backward(): lax.all_gather(held_keys[0], 'ctx', axis=0, tiled=True)  69 us
  transfers between devices with their start and end apart: 33, of which 31 were waited for; matrix products, arithmetic and copies ran while one was open for 13% of the time, Pallas kernels for 0%

profile of v1, /device:TPU:0, one launch (start us, length us, event | category | flops | bytes accessed | tf_op | source)
XLA Modules:
  0.0 2026.5 jit_solution(13351605243480563858)
XLA Ops:
  21.0 42.0 %all-gather.16.cloned.1.call-done = bf16[1024,512]{1,0:T(8,128)(2,1)} async-done(((bf16[128,512]{1,0:T(8,128)(2,1)}), bf16[1024,512]{1,0:T(8,128)(2,1)}) %all-gather.16.cloned.1.call-update) | async-done | bytes 1048592 | tf_op jit(solution)/shard_map/all_gather | solution.py:99
  69.6 34.5 %all-gather.14.cloned.1.call-done = bf16[1024,512]{1,0:T(8,128)(2,1)} async-done(((bf16[128,512]{1,0:T(8,128)(2,1)}), bf16[1024,512]{1,0:T(8,128)(2,1)}) %all-gather.14.cloned.1.call-update) | async-done | bytes 1048592 | tf_op jit(solution)/shard_map/all_gather | solution.py:100
  109.9 22.1 %all-reduce.16.cloned.1.call-done = bf16[128,1024]{1,0:T(8,128)(2,1)} async-done(((bf16[128,1024]{1,0:T(8,128)(2,1)}), bf16[128,1024]{1,0:T(8,128)(2,1)}) %all-reduce.16.cloned.1.call-update) | async-done | bytes 262160 | tf_op jit(solution)/shard_map/psum | solution.py:113
  139.4 23.4 %all-reduce.18.cloned.1.call-done = bf16[128,1024]{1,0:T(8,128)(2,1)} async-done(((bf16[128,1024]{1,0:T(8,128)(2,1)}), bf16[128,1024]{1,0:T(8,128)(2,1)}) %all-reduce.18.cloned.1.call-update) | async-done | bytes 262160 | tf_op jit(solution)/shard_map/psum | solution.py:124
  174.3 39.0 %all-gather.20.cloned.1.call-done = bf16[1024,512]{1,0:T(8,128)(2,1)} async-done(((bf16[128,512]{1,0:T(8,128)(2,1)}), bf16[1024,512]{1,0:T(8,128)(2,1)}) %all-gather.20.cloned.1.call-update) | async-done | bytes 1048592 | tf_op jit(solution)/shard_map/all_gather | solution.py:99
  220.0 34.3 %all-gather.18.cloned.1.call-done = bf16[1024,512]{1,0:T(8,128)(2,1)} async-done(((bf16[128,512]{1,0:T(8,128)(2,1)}), bf16[1024,512]{1,0:T(8,128)(2,1)}) %all-gather.18.cloned.1.call-update) | async-done | bytes 1048592 | tf_op jit(solution)/shard_map/all_gather | solution.py:100
  261.6 21.6 %all-reduce.20.cloned.1.call-done = bf16[128,1024]{1,0:T(8,128)(2,1)} async-done(((bf16[128,1024]{1,0:T(8,128)(2,1)}), bf16[128,1024]{1,0:T(8,128)(2,1)}) %all-reduce.20.cloned.1.call-update) | async-done | bytes 262160 | tf_op jit(solution)/shard_map/psum | solution.py:113
  297.9 28.0 %all-reduce.34.cloned.1.call-done = (bf16[128,1024]{1,0:T(8,128)(2,1)}, bf16[128,1024]{1,0:T(8,128)(2,1)}) async-done(((bf16[128,1024]{1,0:T(8,128)(2,1)}, bf16[128,1024]{1,0:T(8,128)(2,1)}), (bf16[128,1024]{1,0:T(8,128)(2,1)}, bf16[128,1024]{1,0:T(8,128)(2,1)})) %all-reduce.34.cloned.1.call-update) | async-done | bytes 524304 | tf_op jit(solution)/shard_map/psum | solution.py:124
  338.6 30.3 %all-gather.26.cloned.1.call-done = bf16[1024,512]{1,0:T(8,128)(2,1)} async-done(((bf16[128,512]{1,0:T(8,128)(2,1)}), bf16[1024,512]{1,0:T(8,128)(2,1)}) %all-gather.26.cloned.1.call-update) | async-done | bytes 1048592 | tf_op jit(solution)/shard_map/all_gather | solution.py:186
  381.8 28.1 %all-gather.24.cloned.1.call-done = bf16[1024,512]{1,0:T(8,128)(2,1)} async-done(((bf16[128,512]{1,0:T(8,128)(2,1)}), bf16[1024,512]{1,0:T(8,128)(2,1)}) %all-gather.24.cloned.1.call-update) | async-done | bytes 1048592 | tf_op jit(solution)/shard_map/all_gather | solution.py:99
  422.1 29.0 %all-gather.28.cloned.1.call-done = bf16[1024,512]{1,0:T(8,128)(2,1)} async-done(((bf16[128,512]{1,0:T(8,128)(2,1)}), bf16[1024,512]{1,0:T(8,128)(2,1)}) %all-gather.28.cloned.1.call-update) | async-done | bytes 1048592 | tf_op jit(solution)/shard_map/all_gather | solution.py:187
  464.3 27.8 %all-gather.22.cloned.1.call-done = bf16[1024,512]{1,0:T(8,128)(2,1)} async-done(((bf16[128,512]{1,0:T(8,128)(2,1)}), bf16[1024,512]{1,0:T(8,128)(2,1)}) %all-gather.22.cloned.1.call-update) | async-done | bytes 1048592 | tf_op jit(solution)/shard_map/all_gather | solution.py:100
  500.5 58.0 %reduce-scatter.21.cloned.1.call-done = bf16[128,512]{1,0:T(8,128)(2,1)} async-done(((bf16[1024,512]{1,0:T(8,128)(2,1)}), bf16[128,512]{1,0:T(8,128)(2,1)}) %reduce-scatter.21.cloned.1.call-update) | async-done | bytes 131088
  559.5 66.0 %reduce-scatter.19.cloned.1.call-done = bf16[128,512]{1,0:T(8,128)(2,1)} async-done(((bf16[1024,512]{1,0:T(8,128)(2,1)}), bf16[128,512]{1,0:T(8,128)(2,1)}) %reduce-scatter.19.cloned.1.call-update) | async-done | bytes 131088
  631.6 26.0 %all-reduce.32.cloned.1.call-done = (bf16[128,1024]{1,0:T(8,128)(2,1)}, bf16[128,1024]{1,0:T(8,128)(2,1)}) async-done(((bf16[128,1024]{1,0:T(8,128)(2,1)}, bf16[128,1024]{1,0:T(8,128)(2,1)}), (bf16[128,1024]{1,0:T(8,128)(2,1)}, bf16[128,1024]{1,0:T(8,128)(2,1)})) %all-reduce.32.cloned.1.call-update) | async-done | bytes 524304 | tf_op jit(solution)/shard_map/psum | solution.py:113
  678.2 22.3 %all-gather.30.cloned.1.call-done = bf16[1024,512]{1,0:T(8,128)(2,1)} async-done(((bf16[128,512]{1,0:T(8,128)(2,1)}), bf16[1024,512]{1,0:T(8,128)(2,1)}) %all-gather.30.cloned.1.call-update) | async-done | bytes 1048592 | tf_op jit(solution)/shard_map/all_gather | solution.py:186
  706.7 18.5 all-reduce.22.cloned.1.call-done
  738.7 28.8 %all-gather.32.cloned.1.call-done = bf16[1024,512]{1,0:T(8,128)(2,1)} async-done(((bf16[128,512]{1,0:T(8,128)(2,1)}), bf16[1024,512]{1,0:T(8,128)(2,1)}) %all-gather.32.cloned.1.call-update) | async-done | bytes 1048592 | tf_op jit(solution)/shard_map/all_gather | solution.py:187
  784.8 49.6 %reduce-scatter.25.cloned.1.call-done = bf16[128,512]{1,0:T(8,128)(2,1)} async-done(((bf16[1024,512]{1,0:T(8,128)(2,1)}), bf16[128,512]{1,0:T(8,128)(2,1)}) %reduce-scatter.25.cloned.1.call-update) | async-done | bytes 131088
  836.0 64.8 %reduce-scatter.23.cloned.1.call-done = bf16[128,512]{1,0:T(8,128)(2,1)} async-done(((bf16[1024,512]{1,0:T(8,128)(2,1)}), bf16[128,512]{1,0:T(8,128)(2,1)}) %reduce-scatter.23.cloned.1.call-update) | async-done | bytes 131088
  906.7 21.7 %all-reduce.24.cloned.1.call-done = bf16[128,1024]{1,0:T(8,128)(2,1)} async-done(((bf16[128,1024]{1,0:T(8,128)(2,1)}), bf16[128,1024]{1,0:T(8,128)(2,1)}) %all-reduce.24.cloned.1.call-update) | async-done | bytes 262160 | tf_op jit(solution)/shard_map/psum | solution.py:234
  954.5 16.4 all-gather.34.cloned.1.call-done
  977.2 18.5 all-reduce.26.cloned.1.call-done
  1016.2 21.8 %all-gather.36.cloned.1.call-done = bf16[1024,512]{1,0:T(8,128)(2,1)} async-done(((bf16[128,512]{1,0:T(8,128)(2,1)}), bf16[1024,512]{1,0:T(8,128)(2,1)}) %all-gather.36.cloned.1.call-update) | async-done | bytes 1048592 | tf_op jit(solution)/shard_map/all_gather | solution.py:187
  1066.6 37.9 %reduce-scatter.29.cloned.1.call-done = bf16[128,512]{1,0:T(8,128)(2,1)} async-done(((bf16[1024,512]{1,0:T(8,128)(2,1)}), bf16[128,512]{1,0:T(8,128)(2,1)}) %reduce-scatter.29.cloned.1.call-update) | async-done | bytes 131088
  1105.5 66.0 %reduce-scatter.27.cloned.1.call-done = bf16[128,512]{1,0:T(8,128)(2,1)} async-done(((bf16[1024,512]{1,0:T(8,128)(2,1)}), bf16[128,512]{1,0:T(8,128)(2,1)}) %reduce-scatter.27.cloned.1.call-update) | async-done | bytes 131088
  1175.9 9.6 fusion.30
  1211.2 37.3 %all-reduce = (bf16[1,2,512]{2,1,0:T(2,128)(2,1)S(1)}, bf16[1,1024]{1,0:T(2,128)(2,1)S(1)}, bf16[1,2048]{1,0:T(2,128)(2,1)S(1)}, bf16[1,1024]{1,0:T(2,128)(2,1)S...) all-reduce(bf16[1,2,512]{2,1,0:T(2,128)(2,1)S(1)} %fusion.327, ...), channel_id=1, replica_groups=mesh['section'=2,'ctx'=8,'tp'=2] {'ctx'}, use_global_device_ids=true, to_apply=%region_55.56 | all-reduce | flops 9216 | bytes 36864 | tf_op jit(solution)/shard_map/psum | solution.py:327
  1257.5 249.4 %all-reduce.28.cloned.1.call-done = (bf16[1,512,1024]{2,1,0:T(8,128)(2,1)}, bf16[1,1024,2048]{2,1,0:T(8,128)(2,1)}, bf16[1,2048,1024]{2,1,0:T(8,128)(2,1)}) async-done(((bf16[1,512,1024]{2,1,0:T(8,128)(2,1)}, bf16[1,1024,2048]{2,1,0:T(8,128)(2,1)}, bf16[1,2048,1024]{2,1,0:T(8,128)(2,1)}), (bf16[1,512,1024]{2,1,0:T(8,128)(2,1)}, bf16[1,1024,2048]{2,1,0:T(8,128)(2,1)}, ...) | async-done | bytes 9437200 | tf_op jit(solution)/shard_map/psum | solution.py:328
  1509.8 7.1 broadcast_in_dim.170
  1521.3 466.6 %all-gather.38.cloned.1.call-done = bf16[8,1024,3,512]{3,1,2,0:T(8,128)(2,1)} async-done(((bf16[1,1024,3,512]{3,1,2,0:T(8,128)(2,1)}), bf16[8,1024,3,512]{3,1,2,0:T(8,128)(2,1)}) %all-gather.38.cloned.1.call-update) | async-done | bytes 25165840 | tf_op jit(solution)/shard_map/all_gather | solution.py:14
  1987.9 15.3 reduce_sum.555
  (593 shorter events, 348.6 us)
Async XLA Ops:
  7.2 55.8 %all-gather.16.cloned.1.call-start = ((), (), s32[]{:S(2)}) async-start(), calls=%async_computation.7 | async-start | bytes 1179648 | tf_op jit(solution)/shard_map/all_gather | solution.py:99
  19.8 84.3 %all-gather.14.cloned.1.call-start = ((), (), s32[]{:S(2)}) async-start(), calls=%async_computation.6 | async-start | bytes 1179648 | tf_op jit(solution)/shard_map/all_gather | solution.py:100
  20.6 111.3 %all-reduce.16.cloned.1.call-start = ((), (), s32[]{:S(2)}) async-start(), calls=%async_computation.8 | async-start | bytes 524288 | tf_op jit(solution)/shard_map/psum | solution.py:113
  109.8 53.0 %all-reduce.18.cloned.1.call-start = ((), (), s32[]{:S(2)}) async-start(), calls=%async_computation.9 | async-start | bytes 524288 | tf_op jit(solution)/shard_map/psum | solution.py:124
  139.4 73.9 %all-gather.20.cloned.1.call-start = ((), (), s32[]{:S(2)}) async-start(), calls=%async_computation.11 | async-start | bytes 1179648 | tf_op jit(solution)/shard_map/all_gather | solution.py:99
  172.9 81.4 %all-gather.18.cloned.1.call-start = ((), (), s32[]{:S(2)}) async-start(), calls=%async_computation.10 | async-start | bytes 1179648 | tf_op jit(solution)/shard_map/all_gather | solution.py:100
  173.5 109.8 %all-reduce.20.cloned.1.call-start = ((), (), s32[]{:S(2)}) async-start(), calls=%async_computation.12 | async-start | bytes 524288 | tf_op jit(solution)/shard_map/psum | solution.py:113
  261.1 64.8 %all-reduce.34.cloned.1.call-start = ((), (), s32[]{:S(2)}) async-start(), calls=%async_computation.34 | async-start | bytes 1048576 | tf_op jit(solution)/shard_map/psum | solution.py:124
  297.1 71.8 %all-gather.26.cloned.1.call-start = ((), (), s32[]{:S(2)}) async-start(), calls=%async_computation.15 | async-start | bytes 1179648 | tf_op jit(solution)/shard_map/all_gather | solution.py:186
  297.9 112.1 %all-gather.24.cloned.1.call-start = ((), (), s32[]{:S(2)}) async-start(), calls=%async_computation.14 | async-start | bytes 1179648 | tf_op jit(solution)/shard_map/all_gather | solution.py:99
  327.8 2.7 collective-permute-start.1
  336.8 114.3 %all-gather.28.cloned.1.call-start = ((), (), s32[]{:S(2)}) async-start(), calls=%async_computation.16 | async-start | bytes 1179648 | tf_op jit(solution)/shard_map/all_gather | solution.py:187
  337.5 154.6 %all-gather.22.cloned.1.call-start = ((), (), s32[]{:S(2)}) async-start(), calls=%async_computation.13 | async-start | bytes 1179648 | tf_op jit(solution)/shard_map/all_gather | solution.py:100
  375.3 183.2 %reduce-scatter.21.cloned.1.call-start = ((), (), s32[]{:S(2)}) async-start(), calls=%async_computation.26 | async-start | bytes 1179648
  421.9 203.6 %reduce-scatter.19.cloned.1.call-start = ((), (), s32[]{:S(2)}) async-start(), calls=%async_computation.25 | async-start | bytes 1179648
  464.2 193.4 %all-reduce.32.cloned.1.call-start = ((), (), s32[]{:S(2)}) async-start(), calls=%async_computation.33 | async-start | bytes 1048576 | tf_op jit(solution)/shard_map/psum | solution.py:113
  629.8 70.6 %all-gather.30.cloned.1.call-start = ((), (), s32[]{:S(2)}) async-start(), calls=%async_computation.18 | async-start | bytes 1179648 | tf_op jit(solution)/shard_map/all_gather | solution.py:186
  631.6 93.6 %all-reduce.22.cloned.1.call-start = ((), (), s32[]{:S(2)}) async-start(), calls=%async_computation.17 | async-start | bytes 524288 | tf_op jit(solution)/shard_map/psum | solution.py:174
  663.0 6.9 collective-permute-start.2
  675.4 92.1 %all-gather.32.cloned.1.call-start = ((), (), s32[]{:S(2)}) async-start(), calls=%async_computation.19 | async-start | bytes 1179648 | tf_op jit(solution)/shard_map/all_gather | solution.py:187
  677.9 156.5 %reduce-scatter.25.cloned.1.call-start = ((), (), s32[]{:S(2)}) async-start(), calls=%async_computation.28 | async-start | bytes 1179648
  738.7 162.1 %reduce-scatter.23.cloned.1.call-start = ((), (), s32[]{:S(2)}) async-start(), calls=%async_computation.27 | async-start | bytes 1179648
  780.7 147.7 %all-reduce.24.cloned.1.call-start = ((), (), s32[]{:S(2)}) async-start(), calls=%async_computation.20 | async-start | bytes 524288 | tf_op jit(solution)/shard_map/psum | solution.py:234
  905.9 64.9 %all-gather.34.cloned.1.call-start = ((), (), s32[]{:S(2)}) async-start(), calls=%async_computation.22 | async-start | bytes 1179648 | tf_op jit(solution)/shard_map/all_gather | solution.py:186
  906.7 89.1 %all-reduce.26.cloned.1.call-start = ((), (), s32[]{:S(2)}) async-start(), calls=%async_computation.21 | async-start | bytes 524288 | tf_op jit(solution)/shard_map/psum | solution.py:174
  933.6 3.7 collective-permute-start.3
  945.8 92.2 %all-gather.36.cloned.1.call-start = ((), (), s32[]{:S(2)}) async-start(), calls=%async_computation.23 | async-start | bytes 1179648 | tf_op jit(solution)/shard_map/all_gather | solution.py:187
  954.4 150.1 %reduce-scatter.29.cloned.1.call-start = ((), (), s32[]{:S(2)}) async-start(), calls=%async_computation.30 | async-start | bytes 1179648
  1009.4 162.1 %reduce-scatter.27.cloned.1.call-start = ((), (), s32[]{:S(2)}) async-start(), calls=%async_computation.29 | async-start | bytes 1179648
  1050.0 158.4 %all-reduce.30.cloned.1.call-start = ((), (), s32[]{:S(2)}) async-start(), calls=%async_computation.32 | async-start | bytes 1048576 | tf_op jit(solution)/shard_map/psum | solution.py:124
  1175.8 331.2 %all-reduce.28.cloned.1.call-start = ((), (), s32[]{:S(2)}) async-start(), calls=%async_computation.31 | async-start | bytes 18874368 | tf_op jit(solution)/shard_map/psum | solution.py:328
  1187.1 800.9 %all-gather.38.cloned.1.call-start = ((), (), s32[]{:S(2)}) async-start(), calls=%async_computation.24 | async-start | bytes 28311552 | tf_op jit(solution)/shard_map/all_gather | solution.py:14
  (168 other events, 4329.2 us)
Sparse Core Ops, SparseCore 0:
  19.9 42.9 all-gather.15
  65.1 38.9 all-gather.13
  109.9 21.9 all-reduce.15
  139.5 23.2 all-reduce.17
  173.0 40.2 all-gather.19
  215.3 38.9 all-gather.17
  261.2 21.9 all-reduce.19
  297.3 28.6 all-reduce.33
  328.6 40.2 all-gather.25
  370.9 38.9 all-gather.23
  412.1 38.9 all-gather.27
  453.1 38.9 all-gather.21
  495.5 62.9 reduce-scatter.20
  562.3 63.1 reduce-scatter.18
  630.0 27.5 all-reduce.31
  660.1 40.2 all-gather.29
  703.1 21.9 all-reduce.21
  727.2 40.2 all-gather.31
  771.4 62.8 reduce-scatter.24
  837.6 63.1 reduce-scatter.22
  906.0 22.3 all-reduce.23
  930.5 40.2 all-gather.33
  973.7 21.9 all-reduce.25
  997.7 40.2 all-gather.35
  1041.4 63.0 reduce-scatter.28
  1108.3 63.1 reduce-scatter.26
  1175.9 27.6 all-reduce.29
  1208.5 298.4 all-reduce.27
  1508.5 479.3 all-gather.37
